TPU v7x, 32 devices: a whole 2x2x4 slice. The times are simulated.
32 devices in a mesh: parts: 2 (over y), off: 4 (over z), depth: 2 (over x), shot: 2 (over core).
Axes of the slice: x: 2, y: 2, z: 4, core: 2. Of those that a mesh axis runs over, the one named last changes fastest.
Arguments:
- image: bfloat16 [64, 32, 32, 256], P('off', None, 'depth'), may hold values from -4 to 4
- offset_of: int32 [64], P('off'), may hold values from 0 to 63, each once
- background: bfloat16 [4, 32, 32, 256], P(('parts', 'shot'), 'off', 'depth'), parts along dimension 0, may hold values from -6 to 6
- wave_now: float32 [4, 32, 32, 256], P(('parts', 'shot'), 'off', 'depth'), parts along dimension 0, may hold values from -6 to 6
- wave_prev: float32 [4, 32, 32, 256], P(('parts', 'shot'), 'off', 'depth'), parts along dimension 0, may hold values from -6 to 6
- courant: float32 [32, 32, 256], P('off', 'depth'), may hold values from 0.02 to 0.15
Outputs:
- wave_next: float32 [4, 32, 32, 256], P(('parts', 'shot'), 'off', 'depth'), parts along dimension 0
There are 2 independent parts, one for each index of `parts`. A program takes and returns all parts, laid end to end along the dimension named above; an argument that names none is the same for every part. Nothing has to cross between parts.
Inputs may be any that keep to these rules, and one draw needn't show every extreme that they name: Each value appears once; image column k holds offset offset_of[k] - 32 cells along x.
All inputs are finite; a program needn't handle non-finite values.
Results may differ from a plain program's by a relative error of at most 0.0003.
Values may be sent and summed in bfloat16 or wider, within the bound.
A program may use at most 64 MiB of HBM per device.

v0:
```python
import functools

import jax
import jax.numpy as jnp
from jax import lax
from jax.experimental import pallas as pl
from jax.experimental.pallas import tpu as pltpu
from jax.sharding import PartitionSpec as P

H = 64
STENCIL = (-205.0 / 72.0, 8.0 / 5.0, -1.0 / 5.0, 8.0 / 315.0, -1.0 / 560.0)
R = 4
LANES = 128
TOP = 32767.0
PIECES = 4
MESH = pl.DeviceIdType.MESH


def kernel(
    n, nd,
    off_ref, img_hbm, bg_hbm, now_hbm, prev_hbm, cour_hbm,
    out_ref,
    img, bg, wext, prev, cour, shift, acc, part_out, part_in, scale_out, scale_in,
    load_sem, img_sem, bg_send, bg_recv, halo_send, halo_recv, p_send, p_recv, s_send, s_recv,
):
    K, _, Z, X = img.shape
    Y = out_ref.shape[1]
    me = lax.axis_index("off")
    dep = lax.axis_index("depth")
    has = {"l": me > 0, "r": me < n - 1, "u": dep > 0, "d": dep < nd - 1}
    near = {"l": {"off": me - 1}, "r": {"off": me + 1},
            "u": {"depth": dep - 1}, "d": {"depth": dep + 1}}

    fin = out_ref.at[0]

    own = wext.at[pl.ds(R, Y), pl.ds(8, Z), :]
    ld_bg = pltpu.make_async_copy(bg_hbm.at[0], bg.at[me], load_sem.at[0])
    ld_now = pltpu.make_async_copy(now_hbm.at[0], own, load_sem.at[1])
    ld_prev = pltpu.make_async_copy(prev_hbm.at[0], prev, load_sem.at[2])
    ld_cour = pltpu.make_async_copy(cour_hbm, cour, load_sem.at[3])
    ld_bg.start()
    ld_now.start()

    def img_load(j):
        rows = pl.ds(j * Y, Y)
        return pltpu.make_async_copy(img_hbm.at[:, rows], img.at[:, rows], img_sem.at[j])

    img_load(me).start()
    for t in range(1, n):
        @pl.when(me - t >= 0)
        def _():
            img_load(me - t).start()

        @pl.when(me + t < n)
        def _():
            img_load(me + t).start()
    ld_prev.start()
    ld_cour.start()

    barrier = pltpu.get_barrier_semaphore()
    for side in "lrud":
        @pl.when(has[side])
        def _():
            pl.semaphore_signal(barrier, inc=1, device_id=near[side], device_id_type=MESH)

    def clear(rows, cols):
        wext[rows, cols, :] = jnp.zeros((rows.size, cols.size, X), jnp.float32)

    edge = {"l": (pl.ds(0, R), pl.ds(8, Z)), "r": (pl.ds(R + Y, R), pl.ds(8, Z)),
            "u": (pl.ds(R, Y), pl.ds(0, 8)), "d": (pl.ds(R, Y), pl.ds(8 + Z, 8))}
    for side in "lrud":
        @pl.when(jnp.logical_not(has[side]))
        def _():
            clear(*edge[side])

    lead = lax.broadcasted_iota(jnp.int32, (X, X), 1) - lax.broadcasted_iota(jnp.int32, (X, X), 0)

    def build(k, carry):
        h = off_ref[k] - H // 2
        shift[k] = jnp.where(lead == h, 1.0, 0.0).astype(jnp.bfloat16)
        return carry

    lax.fori_loop(0, K, build, 0)
    ld_bg.wait()
    ld_now.wait()
    count = sum(has[s].astype(jnp.int32) for s in "lrud")
    pl.semaphore_wait(barrier, count)

    step = Y // PIECES if Y % PIECES == 0 else Y
    pieces = Y // step

    def bg_copy(j, c, target, slot):
        block = bg.at[j, pl.ds(c * step, step)]
        return pltpu.make_async_remote_copy(
            src_ref=block, dst_ref=block, send_sem=bg_send.at[slot, j * pieces + c],
            recv_sem=bg_recv.at[j * pieces + c], device_id={"off": target},
            device_id_type=MESH)

    mine = {"l": (pl.ds(R, R), pl.ds(8, Z)), "r": (pl.ds(Y, R), pl.ds(8, Z)),
            "u": (pl.ds(R, Y), pl.ds(8, 8)), "d": (pl.ds(R, Y), pl.ds(Z, 8))}
    other = {"l": "r", "r": "l", "u": "d", "d": "u"}
    num = {"l": 0, "r": 1, "u": 2, "d": 3}

    def halo_copy(side):
        there = other[side]
        return pltpu.make_async_remote_copy(
            src_ref=wext.at[mine[side][0], mine[side][1], :],
            dst_ref=wext.at[edge[there][0], edge[there][1], :],
            send_sem=halo_send.at[num[side]], recv_sem=halo_recv.at[num[there]],
            device_id=near[side], device_id_type=MESH)

    for c in range(pieces):
        for slot, side in enumerate("lr"):
            @pl.when(has[side])
            def _():
                bg_copy(me, c, near[side]["off"], slot).start()
    for side in "lrud":
        @pl.when(has[side])
        def _():
            halo_copy(side).start()


    group = 4 if K % 4 == 0 else 1

    def partial(j, dst, slot):
        lhs = bg[j].reshape(Y * Z, X)
        rows = pl.ds(j * Y, Y)

        def body(g, carry):
            total = None
            for m in range(group):
                k = g * group + m
                moved = jnp.dot(lhs, shift[k], preferred_element_type=jnp.float32)
                term = img[k, rows].astype(jnp.float32) * moved.reshape(Y, Z, X)
                total = term if total is None else total + term

            @pl.when(g == 0)
            def _():
                dst[slot] = total

            @pl.when(g > 0)
            def _():
                dst[slot] = dst[slot] + total
            return carry

        lax.fori_loop(0, K // group, body, 0)

    def fold(full):
        top = jnp.max(full, axis=0)
        rows8 = functools.reduce(jnp.maximum, [top[z : z + 8] for z in range(0, Z, 8)])
        return functools.reduce(
            jnp.maximum, [rows8[:, x : x + LANES] for x in range(0, X, LANES)])

    def spread(small):
        return jnp.concatenate(
            [jnp.concatenate([small] * (X // LANES), axis=1)] * (Z // 8), axis=0)

    def encode(j):
        top = fold(jnp.abs(acc[1]))
        scale_out[j] = top * (1.0 / TOP)
        up = spread(jnp.where(top > 0.0, TOP / top, 0.0))
        for y in range(Y):
            whole = jnp.round(jnp.clip(acc[1, y] * up, -TOP, TOP)).astype(jnp.int32)
            part_out[j, y] = whole.astype(jnp.int16)

    def decoded(j):
        down = spread(scale_in[j])
        return part_in[j].astype(jnp.int32).astype(jnp.float32) * down[None]

    def part_copies(j, slot):
        return [
            pltpu.make_async_remote_copy(
                src_ref=src.at[j], dst_ref=dst.at[slot], send_sem=send.at[j],
                recv_sem=recv.at[slot], device_id={"off": j}, device_id_type=MESH)
            for src, dst, send, recv in (
                (scale_out, scale_in, s_send, s_recv), (part_out, part_in, p_send, p_recv))
        ]

    def arrivals(t):
        return ((me - t, me - t >= 0, 1), (me + t, me + t < n, -1))

    def onward(t, sign):
        if t % 2 == 0:
            return ()
        spots = [(me + hop * sign, slot) for slot, hop in ((1, 2), (0, 1))]
        return [(to, jnp.logical_and(to >= 0, to < n), slot) for to, slot in spots]

    img_load(me).wait()
    partial(me, acc, 0)

    def send_partial(j, ok):
        @pl.when(ok)
        def _():
            img_load(j).wait()
            partial(j, acc, 1)
            encode(j)
            for copy in part_copies(j, me):
                copy.start()

    order = [1] + [t for low in range(2, n, 2) for t in (low + 1, low) if t < n]
    for t in order:
        for c in range(pieces):
            for j, ok, sign in arrivals(t):
                @pl.when(ok)
                def _():
                    bg_copy(j, c, me, 0).wait_recv()
            for j, ok, sign in arrivals(t):
                for to, there, slot in onward(t, sign):
                    @pl.when(jnp.logical_and(ok, there))
                    def _():
                        bg_copy(j, c, to, slot).start()
        for j, ok, sign in arrivals(t):
            send_partial(j, ok)

    ld_prev.wait()
    ld_cour.wait()
    for side in "lrud":
        @pl.when(has[side])
        def _():
            halo_copy(side).wait_send()
            pltpu.make_async_remote_copy(
                src_ref=wext.at[mine[side][0], mine[side][1], :],
                dst_ref=wext.at[edge[side][0], edge[side][1], :],
                send_sem=halo_send.at[num[side]], recv_sem=halo_recv.at[num[side]],
                device_id=near[side], device_id_type=MESH).wait_recv()

    lane = lax.broadcasted_iota(jnp.int32, (Z, X), 1)

    def plane(y, carry):
        centre = wext[y + R, pl.ds(8, Z), :]
        running = 3.0 * STENCIL[0] * centre
        for r in range(1, R + 1):
            beside = wext[y + R + r, pl.ds(8, Z), :] + wext[y + R - r, pl.ds(8, Z), :]
            beside = beside + wext[y + R, pl.ds(8 + r, Z), :]
            beside = beside + wext[y + R, pl.ds(8 - r, Z), :]
            beside = beside + jnp.where(lane < X - r, pltpu.roll(centre, X - r, 1), 0.0)
            beside = beside + jnp.where(lane >= r, pltpu.roll(centre, r, 1), 0.0)
            running = running + STENCIL[r] * beside
        fin[y] = 2.0 * centre - prev[y] + cour[y] * (running + acc[0, y])
        return carry

    lax.fori_loop(0, Y, plane, 0)

    for t in range(1, n):
        for j, ok in ((me - t, me - t >= 0), (me + t, me + t < n)):
            @pl.when(ok)
            def _():
                for copy in part_copies(j, j):
                    copy.wait_recv()
                fin[...] = fin[...] + cour[...] * decoded(j)

    for c in range(pieces):
        for slot, side in enumerate("lr"):
            @pl.when(has[side])
            def _():
                bg_copy(me, c, near[side]["off"], slot).wait_send()
    for t in range(1, n):
        for j, ok, sign in arrivals(t):
            @pl.when(ok)
            def _():
                for copy in part_copies(j, me):
                    copy.wait_send()
            for to, there, slot in onward(t, sign):
                @pl.when(jnp.logical_and(ok, there))
                def _():
                    for c in range(pieces):
                        bg_copy(j, c, to, slot).wait_send()


def on_device(n, nd, image, offset_of, background, wave_now, wave_prev, courant):
    K, rows, Z, X = image.shape
    Y = wave_now.shape[1]
    f32 = jnp.float32
    anywhere = pl.BlockSpec(memory_space=pltpu.HBM)
    dma = pltpu.SemaphoreType.DMA
    return pl.pallas_call(
        functools.partial(kernel, n, nd),
        out_shape=jax.ShapeDtypeStruct(wave_now.shape, f32),
        in_specs=[pl.BlockSpec(memory_space=pltpu.SMEM)] + [anywhere] * 5,
        out_specs=pl.BlockSpec(memory_space=pltpu.VMEM),
        scratch_shapes=[
            pltpu.VMEM((K, rows, Z, X), jnp.bfloat16),
            pltpu.VMEM((n, Y, Z, X), jnp.bfloat16),
            pltpu.VMEM((Y + 2 * R, Z + 16, X), f32),
            pltpu.VMEM((Y, Z, X), f32),
            pltpu.VMEM((Y, Z, X), f32),
            pltpu.VMEM((K, X, X), jnp.bfloat16),
            pltpu.VMEM((2, Y, Z, X), f32),
            pltpu.VMEM((n, Y, Z, X), jnp.int16),
            pltpu.VMEM((n, Y, Z, X), jnp.int16),
            pltpu.VMEM((n, 8, LANES), f32),
            pltpu.VMEM((n, 8, LANES), f32),
            dma((4,)), dma((n,)), dma((2, n * PIECES)), dma((n * PIECES,)), dma((4,)), dma((4,)),
            dma((n,)), dma((n,)), dma((n,)), dma((n,)),
        ],
        compiler_params=pltpu.CompilerParams(
            collective_id=0, has_side_effects=True, vmem_limit_bytes=50331648),
        name="born_step",
    )(*[pltpu.with_memory_space_constraint(a, pltpu.HBM) for a in
        (offset_of, image, background, wave_now, wave_prev, courant)])


def solution(mesh):
    wave = P(("parts", "shot"), "off", "depth", None)
    return jax.shard_map(
        functools.partial(on_device, mesh.shape["off"], mesh.shape["depth"]),
        mesh=mesh,
        in_specs=(
            P("off", None, "depth", None),
            P("off"),
            wave,
            wave,
            wave,
            P("off", "depth", None),
        ),
        out_specs=wave,
        check_vma=False,
    )
```

profile of v0, /device:TPU:0, one launch (start us, length us, event | category | flops | bytes accessed | tf_op | source)
XLA Modules:
  0.0 20.7 jit_solution(4187095327269337599)
XLA Ops:
  0.0 20.1 %born_step.1 = f32[1,8,16,256]{3,2,1,0:T(8,128)S(1)} custom-call(s32[16]{0:T(128)} %off_ref.1, bf16[16,32,16,256]{3,2,1,0:T(8,128)(2,1)} %img_hbm.1, bf16[1,8,16,256]{3,2,1,0:T(8,128)(2,1)} %bg_hbm.1, f32[1,8,16,256]{3,2,1,0:T(8,128)} %now_hbm.1, f32[1,8,16,256]{3,2,1,0:T(8,128)} %prev_hbm.1, f32[8,16,256]{2,1,0:T(8,128)} %cour_hbm.1), custom_call_target="tpu_custom_call" | custom-call | tf_op jit(solution)/shard_map/born_step/pallas_call | solution.py:276
  20.1 0.7 %copy.8 = f32[1,8,16,256]{3,2,1,0:T(8,128)} copy(f32[1,8,16,256]{3,2,1,0:T(8,128)S(1)} %born_step.1) | data formatting | bytes 262144
where the time goes:
time: 20.9 us; the launch traced here: 20.7 us
  Pallas kernels  20.1 us (96%)
  local copies, waits for them, and re-layouts  0.66 us (3%)
    pallas_call x1, Pallas kernels, on_device(): pl.pallas_call(functools.partial(kernel, n, nd), out_shape=jax.ShapeDtype...  20.1 us
    unnamed x1, local copies, waits for them, and re-layouts  0.66 us

commit v1 on v0

--- a/solution.py
+++ b/solution.py
@@ -18,10 +18,10 @@
 
 def kernel(
     n, nd,
-    off_ref, img_hbm, bg_hbm, now_hbm, prev_hbm, cour_hbm,
+    off_hbm, img_hbm, bg_hbm, now_hbm, prev_hbm, cour_hbm,
     out_ref,
     img, bg, wext, prev, cour, shift, acc, part_out, part_in, scale_out, scale_in,
-    load_sem, img_sem, bg_send, bg_recv, halo_send, halo_recv, p_send, p_recv, s_send, s_recv,
+    off_ref, load_sem, img_sem, bg_send, bg_recv, halo_send, halo_recv, p_send, p_recv, s_send, s_recv,
 ):
     K, _, Z, X = img.shape
     Y = out_ref.shape[1]
@@ -38,6 +38,8 @@
     ld_now = pltpu.make_async_copy(now_hbm.at[0], own, load_sem.at[1])
     ld_prev = pltpu.make_async_copy(prev_hbm.at[0], prev, load_sem.at[2])
     ld_cour = pltpu.make_async_copy(cour_hbm, cour, load_sem.at[3])
+    ld_off = pltpu.make_async_copy(off_hbm, off_ref, load_sem.at[4])
+    ld_off.start()
     ld_bg.start()
     ld_now.start()
 
@@ -80,6 +82,7 @@
         shift[k] = jnp.where(lead == h, 1.0, 0.0).astype(jnp.bfloat16)
         return carry
 
+    ld_off.wait()
     lax.fori_loop(0, K, build, 0)
     ld_bg.wait()
     ld_now.wait()
@@ -122,28 +125,34 @@
 
     group = 4 if K % 4 == 0 else 1
 
+    lane1 = lax.broadcasted_iota(jnp.int32, (8, LANES), 1)
+
     def partial(j, dst, slot):
-        lhs = bg[j].reshape(Y * Z, X)
-        rows = pl.ds(j * Y, Y)
-
-        def body(g, carry):
-            total = None
-            for m in range(group):
-                k = g * group + m
-                moved = jnp.dot(lhs, shift[k], preferred_element_type=jnp.float32)
-                term = img[k, rows].astype(jnp.float32) * moved.reshape(Y, Z, X)
-                total = term if total is None else total + term
-
-            @pl.when(g == 0)
-            def _():
-                dst[slot] = total
-
-            @pl.when(g > 0)
-            def _():
-                dst[slot] = dst[slot] + total
+        def body(y, carry):
+            for zt in range(Z // 8):
+                src = bg[j, y, :, :].astype(jnp.float32)[zt * 8 : zt * 8 + 8]
+                half = H // 2
+                zero = jnp.zeros((8, LANES), jnp.float32)
+                tiles = [pltpu.roll(src[:, x : x + LANES], half, 1) for x in range(0, X, LANES)]
+                ext = []
+                for q in range(X // LANES + 1):
+                    lo = tiles[q - 1] if q > 0 else zero
+                    hi = tiles[q] if q < X // LANES else zero
+                    ext.append(jnp.where(lane1 < half, lo, hi))
+                acc_t = [None] * (X // LANES)
+                for k in range(K):
+                    o = half - (off_ref[k] - half)
+                    r = [pltpu.roll(t, LANES - o, 1) for t in ext]
+                    keep = lane1 < LANES - o
+                    im = img[k, j * Y + y].astype(jnp.float32)[zt * 8 : zt * 8 + 8]
+                    for q in range(X // LANES):
+                        moved = jnp.where(keep, r[q], r[q + 1])
+                        term = im[:, q * LANES : q * LANES + LANES] * moved
+                        acc_t[q] = term if acc_t[q] is None else acc_t[q] + term
+                dst[slot, y, pl.ds(zt * 8, 8), :] = jnp.concatenate(acc_t, axis=1)
             return carry
 
-        lax.fori_loop(0, K // group, body, 0)
+        lax.fori_loop(0, Y, body, 0)
 
     def fold(full):
         top = jnp.max(full, axis=0)
@@ -246,7 +255,7 @@
             @pl.when(ok)
             def _():
                 for copy in part_copies(j, j):
-                    copy.wait_recv()
+                  copy.wait_recv()
                 fin[...] = fin[...] + cour[...] * decoded(j)
 
     for c in range(pieces):
@@ -276,7 +285,7 @@
     return pl.pallas_call(
         functools.partial(kernel, n, nd),
         out_shape=jax.ShapeDtypeStruct(wave_now.shape, f32),
-        in_specs=[pl.BlockSpec(memory_space=pltpu.SMEM)] + [anywhere] * 5,
+        in_specs=[anywhere] * 6,
         out_specs=pl.BlockSpec(memory_space=pltpu.VMEM),
         scratch_shapes=[
             pltpu.VMEM((K, rows, Z, X), jnp.bfloat16),
@@ -290,7 +299,7 @@
             pltpu.VMEM((n, Y, Z, X), jnp.int16),
             pltpu.VMEM((n, 8, LANES), f32),
             pltpu.VMEM((n, 8, LANES), f32),
-            dma((4,)), dma((n,)), dma((2, n * PIECES)), dma((n * PIECES,)), dma((4,)), dma((4,)),
+            pltpu.SMEM((K,), jnp.int32), dma((5,)), dma((n,)), dma((2, n * PIECES)), dma((n * PIECES,)), dma((4,)), dma((4,)),
             dma((n,)), dma((n,)), dma((n,)), dma((n,)),
         ],
         compiler_params=pltpu.CompilerParams(

time: 20.9 us -> 20.3 us (0.971)
  Pallas kernels: 20.1 us -> 19.5 us
    pallas_call x1, Pallas kernels: 20.1 us -> 19.5 us  [on_device(): pl.pallas_call(functools.partial(kernel, n, nd), out_shape=jax.ShapeDtype...]
where the time goes in v1:
time: 20.3 us; the launch traced here: 20.2 us
  Pallas kernels  19.5 us (96%)
  local copies, waits for them, and re-layouts  0.66 us (3%)
    pallas_call x1, Pallas kernels, on_device(): pl.pallas_call(functools.partial(kernel, n, nd), out_shape=jax.ShapeDtype...  19.5 us
    unnamed x1, local copies, waits for them, and re-layouts  0.66 us

profile of v1, /device:TPU:0, one launch (start us, length us, event | category | flops | bytes accessed | tf_op | source)
XLA Modules:
  0.0 20.2 jit_solution(13646117450826772561)
XLA Ops:
  0.0 19.5 %born_step.1 = f32[1,8,16,256]{3,2,1,0:T(8,128)S(1)} custom-call(s32[16]{0:T(128)} %off_hbm.1, bf16[16,32,16,256]{3,2,1,0:T(8,128)(2,1)} %img_hbm.1, bf16[1,8,16,256]{3,2,1,0:T(8,128)(2,1)} %bg_hbm.1, f32[1,8,16,256]{3,2,1,0:T(8,128)} %now_hbm.1, f32[1,8,16,256]{3,2,1,0:T(8,128)} %prev_hbm.1, f32[8,16,256]{2,1,0:T(8,128)} %cour_hbm.1), custom_call_target="tpu_custom_call" | custom-call | tf_op jit(solution)/shard_map/born_step/pallas_call | solution.py:285
  19.5 0.7 %copy.8 = f32[1,8,16,256]{3,2,1,0:T(8,128)} copy(f32[1,8,16,256]{3,2,1,0:T(8,128)S(1)} %born_step.1) | data formatting | bytes 262144

commit v2 on v0

v2 whole, which is shorter than its diff:
```python
import functools

import jax
import jax.numpy as jnp
from jax import lax
from jax.experimental import pallas as pl
from jax.experimental.pallas import tpu as pltpu
from jax.sharding import PartitionSpec as P

STENCIL = (-205.0 / 72.0, 8.0 / 5.0, -1.0 / 5.0, 8.0 / 315.0, -1.0 / 560.0)
R = 4
LANES = 128
TOP = 32767.0
PIECES = 2
MESH = pl.DeviceIdType.MESH


def kernel(
    n, nd,
    off_hbm, img_hbm, bg_hbm, now_hbm, prev_hbm, cour_hbm,
    out_ref,
    off_ref, img, raw, bg, wext, prev, cour, shift, acc,
    part_out, part_in, scale_out, scale_in, tally,
    edge_out, edge_in, edge_scale_out, edge_scale_in, edge_tally,
    load_sem, img_sem, ready, near_ready, bg_recv, bg_send, fwd_send,
    halo_send, halo_recv, p_recv, p_send,
):
    K, _, Z, X = img.shape
    Y = out_ref.shape[1]
    step = part_out.shape[2]
    pieces = part_out.shape[1]
    half = K * n // 2
    me = lax.axis_index("off")
    dep = lax.axis_index("depth")
    other_shot = lax.axis_size("shot") - 1 - lax.axis_index("shot")
    has = {"l": me > 0, "r": me < n - 1, "u": dep > 0, "d": dep < nd - 1}
    near = {"l": {"off": me - 1}, "r": {"off": me + 1},
            "u": {"depth": dep - 1}, "d": {"depth": dep + 1}}
    fin = out_ref.at[0]

    def far(j):
        return {"off": j, "shot": other_shot}

    ld_bg = pltpu.make_async_copy(bg_hbm.at[0], raw, load_sem.at[0])
    ld_off = pltpu.make_async_copy(off_hbm, off_ref, load_sem.at[1])
    ld_now = pltpu.make_async_copy(
        now_hbm.at[0], wext.at[pl.ds(R, Y), pl.ds(8, Z), :], load_sem.at[2])
    ld_prev = pltpu.make_async_copy(prev_hbm.at[0], prev, load_sem.at[3])
    ld_cour = pltpu.make_async_copy(cour_hbm, cour, load_sem.at[4])
    ld_bg.start()
    ld_off.start()
    ld_now.start()

    barrier = pltpu.get_barrier_semaphore()
    for t in range(1, n):
        @pl.when(me + t < n)
        def _():
            pl.semaphore_signal(barrier, inc=1, device_id=far(me + t), device_id_type=MESH)
    for side in "rd":
        @pl.when(has[side])
        def _():
            pl.semaphore_signal(barrier, inc=1, device_id=near[side], device_id_type=MESH)

    def img_load(j):
        rows = pl.ds(j * Y, Y)
        return pltpu.make_async_copy(img_hbm.at[:, rows], img.at[:, rows], img_sem.at[j])

    def order(i):
        last = me == n - 1
        rest = jnp.where(jnp.logical_or(i - 1 < me, last), i - 1, i + 1)
        first = jnp.where(last, me - 1, me + 1)
        high = jnp.where(i == 0, first, jnp.where(i == 1, 0, rest))
        low = jnp.where(jnp.logical_and(i == 0, me == 1), 0, i + 1)
        return jnp.where(me < 2, low, high)

    img_load(me).start()

    @pl.loop(0, n - 1)
    def _(i):
        img_load(order(i)).start()

    ld_prev.start()
    ld_cour.start()

    def clear(rows, cols):
        wext[rows, cols, :] = jnp.zeros((rows.size, cols.size, X), jnp.float32)

    edge = {"l": (pl.ds(0, R), pl.ds(8, Z)), "r": (pl.ds(R + Y, R), pl.ds(8, Z)),
            "u": (pl.ds(R, Y), pl.ds(0, 8)), "d": (pl.ds(R, Y), pl.ds(8 + Z, 8))}
    for side in "lrud":
        @pl.when(jnp.logical_not(has[side]))
        def _():
            clear(*edge[side])

    mine = {"l": pl.ds(R, R), "r": pl.ds(Y, R), "u": pl.ds(0, 8), "d": pl.ds(Z - 8, 8)}
    other = {"l": "r", "r": "l", "u": "d", "d": "u"}
    num = {"l": 0, "r": 1, "u": 2, "d": 3}

    def halo_copies(side):
        there = other[side]
        if side in "ud":
            pairs = [(now_hbm.at[0, :, mine[side], :], wext.at[edge[there][0], edge[there][1], :])]
        else:
            pairs = [(edge_out.at[num[side]], edge_in.at[num[there]]),
                     (edge_scale_out.at[num[side]], edge_scale_in.at[num[there]])]
        return [
            pltpu.make_async_remote_copy(
                src_ref=src, dst_ref=dst, send_sem=halo_send.at[num[side]],
                recv_sem=halo_recv.at[num[there]], device_id=near[side], device_id_type=MESH)
            for src, dst in pairs
        ]

    def halo_wait(side, sem):
        if side in "ud":
            there = wext.at[edge[side][0], edge[side][1], :]
            pltpu.make_async_copy(there, there, sem.at[num[side]]).wait()
        else:
            pltpu.make_async_copy(edge_tally, edge_tally, sem.at[num[side]]).wait()

    lower = me + has["l"].astype(jnp.int32) + has["u"].astype(jnp.int32)

    @pl.when(lower > 0)
    def _():
        pl.semaphore_wait(barrier, lower)
    for t in range(n - 1, 0, -1):
        @pl.when(me - t >= 0)
        def _():
            pl.semaphore_signal(ready.at[me], inc=1, device_id=far(me - t), device_id_type=MESH)
    for side, slot in (("l", 0), ("u", 1)):
        @pl.when(has[side])
        def _():
            pl.semaphore_signal(near_ready.at[slot], inc=1, device_id=near[side], device_id_type=MESH)

    @pl.when(has["u"])
    def _():
        for copy in halo_copies("u"):
            copy.start()

    tiles = X // LANES

    def encode(total, whole_ref, scale_ref, *at):
        top = jnp.max(jnp.abs(total), axis=(0, 1))[None]
        top = functools.reduce(
            jnp.maximum, [top[:, q * LANES : (q + 1) * LANES] for q in range(tiles)])
        scale_ref[at] = top * (1.0 / TOP)
        up = jnp.concatenate([jnp.where(top > 0.0, TOP / top, 0.0)] * tiles, axis=1)
        whole = jnp.round(jnp.clip(total * up[None], -TOP, TOP)).astype(jnp.int32)
        whole_ref[at] = whole.astype(jnp.int16)

    def decode(whole_ref, scale_ref, *at):
        down = jnp.concatenate([scale_ref[at]] * tiles, axis=1)
        return whole_ref[at].astype(jnp.int32).astype(jnp.float32) * down[None]

    ld_bg.wait()
    for y in range(Y):
        bg[me, y] = pltpu.roll(raw[y].astype(jnp.float32), half, 1).astype(jnp.bfloat16)

    def piece_of(j, c):
        return bg.at[j, pl.ds(c * step, step)]

    def bg_copy(j, c, target, send):
        return pltpu.make_async_remote_copy(
            src_ref=piece_of(j, c), dst_ref=piece_of(j, c), send_sem=send,
            recv_sem=bg_recv.at[j * pieces + c], device_id=target, device_id_type=MESH)

    def bg_sent(j, target, send):
        return pltpu.make_async_remote_copy(
            src_ref=bg.at[j], dst_ref=bg.at[j], send_sem=send,
            recv_sem=bg_recv.at[j * pieces], device_id=target, device_id_type=MESH)

    def relayed(j, g):
        return jnp.logical_and(j >= 1, g >= j + 2)

    def direct(g):
        ok = jnp.logical_and(g >= 0, g < n)
        return jnp.logical_and(ok, jnp.logical_not(relayed(me, g)))

    def send_own(g):
        for c in range(pieces):
            bg_copy(me, c, far(g), bg_send.at[g]).start()

    for t in range(1, n):
        @pl.when(direct(me - t))
        def _():
            send_own(me - t)

    ld_now.wait()
    for side in "lr":
        encode(wext[mine[side], pl.ds(8, Z), :], edge_out, edge_scale_out, num[side])

    @pl.when(has["l"])
    def _():
        for copy in halo_copies("l"):
            copy.start()

    lead = lax.broadcasted_iota(jnp.int32, (2 * LANES, LANES), 0) - lax.broadcasted_iota(
        jnp.int32, (2 * LANES, LANES), 1)
    ld_off.wait()
    for k in range(K):
        move = 2 * half - off_ref[k]
        shift[k // 2, :, pl.ds(k % 2 * LANES, LANES)] = jnp.where(
            lead == move, 1.0, 0.0).astype(jnp.bfloat16)

    lane = lax.broadcasted_iota(jnp.int32, (step * Z, LANES), 1)

    def partial(j, c):
        rows = bg[j, pl.ds(c * step, step)].reshape(step * Z, X)
        cols = [rows[:, q * LANES : (q + 1) * LANES] for q in range(tiles)]
        zero = jnp.zeros_like(cols[0])
        cols.append(jnp.where(lane < half, cols[0], zero))
        cols[0] = jnp.where(lane < half, zero, cols[0])
        lhs = jnp.concatenate(
            [jnp.concatenate([cols[q], cols[q + 1]], axis=1) for q in range(tiles)], axis=0)
        total = None
        for k in range(K):
            if k % 2 == 0:
                moved = jnp.dot(lhs, shift[k // 2], preferred_element_type=jnp.float32)
            side = moved[:, k % 2 * LANES : (k % 2 + 1) * LANES]
            line = jnp.concatenate(
                [side[q * step * Z : (q + 1) * step * Z] for q in range(tiles)], axis=1)
            term = img[k, pl.ds(j * Y + c * step, step)].astype(jnp.float32) * line.reshape(step, Z, X)
            total = term if total is None else total + term
        return total

    def part_send(j, c):
        for s, (src, dst) in enumerate(((part_out, part_in), (scale_out, scale_in))):
            pltpu.make_async_remote_copy(
                src_ref=src.at[j, c], dst_ref=dst.at[me, c], send_sem=p_send.at[s],
                recv_sem=p_recv.at[me], device_id=far(j), device_id_type=MESH).start()

    img_load(me).wait()
    for c in range(pieces):
        acc[pl.ds(c * step, step)] = partial(me, c)

    for t in range(1, n):
        @pl.when(direct(me + t))
        def _():
            pl.semaphore_wait(ready.at[me + t], 1)
            send_own(me + t)
    @pl.when(has["d"])
    def _():
        pl.semaphore_wait(near_ready.at[1], 1)
        for copy in halo_copies("d"):
            copy.start()

    @pl.when(has["r"])
    def _():
        pl.semaphore_wait(near_ready.at[0], 1)
        for copy in halo_copies("r"):
            copy.start()

    @pl.loop(0, n - 1)
    def _(i):
        j = order(i)

        onward = jnp.where(j < me, me + 1, me - 1)
        go_on = jnp.logical_and(
            jnp.logical_and(onward >= 0, onward < n), relayed(j, onward))
        for c in range(pieces):
            bg_copy(j, c, far(j), bg_send.at[j]).wait_recv()

            @pl.when(go_on)
            def _():
                bg_copy(j, c, {"off": onward}, fwd_send.at[j]).start()

            if c == 0:
                img_load(j).wait()

                @pl.when(jnp.logical_and(j > me, relayed(me, j)))
                def _():
                    pl.semaphore_wait(ready.at[j], 1)
            encode(partial(j, c), part_out, scale_out, j, c)
            part_send(j, c)

    ld_prev.wait()
    ld_cour.wait()
    for side in "lrud":
      @pl.when(has[side])
      def _():
          halo_wait(side, halo_recv)
          if side in "lr":
              wext[edge[side][0], edge[side][1], :] = decode(edge_in, edge_scale_in, num[side])

    wide = lax.broadcasted_iota(jnp.int32, (Z, X), 1)

    def plane(y, carry):
        centre = wext[y + R, pl.ds(8, Z), :]
        running = 3.0 * STENCIL[0] * centre
        for r in range(1, R + 1):
            beside = wext[y + R + r, pl.ds(8, Z), :] + wext[y + R - r, pl.ds(8, Z), :]
            beside = beside + wext[y + R, pl.ds(8 + r, Z), :]
            beside = beside + wext[y + R, pl.ds(8 - r, Z), :]
            beside = beside + jnp.where(wide < X - r, pltpu.roll(centre, X - r, 1), 0.0)
            beside = beside + jnp.where(wide >= r, pltpu.roll(centre, r, 1), 0.0)
            running = running + STENCIL[r] * beside
        fin[y] = 2.0 * centre - prev[y] + cour[y] * (running + acc[y])
        return carry

    lax.fori_loop(0, Y, plane, 0)

    @pl.loop(0, n - 1)
    def _(i):
        j = order(i)

        pltpu.make_async_copy(tally, tally, p_recv.at[j]).wait()
        for c in range(pieces):
            rows = pl.ds(c * step, step)
            fin[rows] = fin[rows] + cour[rows] * decode(part_in, scale_in, j, c)

    for side in "lrud":
      @pl.when(has[side])
      def _():
          halo_wait(side, halo_send)
    for t in range(1, n):
      for g in (me - t, me + t):
          @pl.when(direct(g))
          def _():
              bg_sent(me, far(g), bg_send.at[g]).wait_send()

    @pl.loop(0, n - 1)
    def _(i):
      j = order(i)
      onward = jnp.where(j < me, me + 1, me - 1)
      go_on = jnp.logical_and(
          jnp.logical_and(onward >= 0, onward < n), relayed(j, onward))

      @pl.when(go_on)
      def _():
          bg_sent(j, {"off": onward}, fwd_send.at[j]).wait_send()

    for s, src in enumerate((part_out, scale_out)):
      sent = src.at[pl.ds(0, n - 1)]
      pltpu.make_async_copy(sent, sent, p_send.at[s]).wait()


def on_device(n, nd, image, offset_of, background, wave_now, wave_prev, courant):
    K, rows, Z, X = image.shape
    Y = wave_now.shape[1]
    f32 = jnp.float32
    pieces = PIECES if Y % PIECES == 0 else 1
    step = Y // pieces
    lines = (Y * Z * X * 2) // (LANES * 4) + pieces
    dma = pltpu.SemaphoreType.DMA
    regular = pltpu.SemaphoreType.REGULAR
    return pl.pallas_call(
        functools.partial(kernel, n, nd),
        out_shape=jax.ShapeDtypeStruct(wave_now.shape, f32),
        in_specs=[pl.BlockSpec(memory_space=pltpu.HBM)] * 6,
        out_specs=pl.BlockSpec(memory_space=pltpu.VMEM),
        scratch_shapes=[
            pltpu.SMEM((K,), jnp.int32),
            pltpu.VMEM((K, rows, Z, X), jnp.bfloat16),
            pltpu.VMEM((Y, Z, X), jnp.bfloat16),
            pltpu.VMEM((n, Y, Z, X), jnp.bfloat16),
            pltpu.VMEM((Y + 2 * R, Z + 16, X), f32),
            pltpu.VMEM((Y, Z, X), f32),
            pltpu.VMEM((Y, Z, X), f32),
            pltpu.VMEM(((K + 1) // 2, 2 * LANES, 2 * LANES), jnp.bfloat16),
            pltpu.VMEM((Y, Z, X), f32),
            pltpu.VMEM((n, pieces, step, Z, X), jnp.int16),
            pltpu.VMEM((n, pieces, step, Z, X), jnp.int16),
            pltpu.VMEM((n, pieces, 1, LANES), f32),
            pltpu.VMEM((n, pieces, 1, LANES), f32),
            pltpu.VMEM((lines, LANES), f32),
            pltpu.VMEM((2, R, Z, X), jnp.int16),
            pltpu.VMEM((2, R, Z, X), jnp.int16),
            pltpu.VMEM((2, 1, LANES), f32),
            pltpu.VMEM((2, 1, LANES), f32),
            pltpu.VMEM(((R * Z * X * 2) // (LANES * 4) + 1, LANES), f32),
            dma((5,)), dma((n,)), regular((n,)), regular((2,)),
            dma((n * pieces,)), dma((n,)), dma((n,)),
            dma((4,)), dma((4,)), dma((n,)), dma((2,)),
        ],
        compiler_params=pltpu.CompilerParams(
            collective_id=0, has_side_effects=True, vmem_limit_bytes=50331648),
        name="born_step",
    )(*[pltpu.with_memory_space_constraint(a, pltpu.HBM) for a in
        (offset_of, image, background, wave_now, wave_prev, courant)])


def solution(mesh):
    wave = P(("parts", "shot"), "off", "depth", None)
    return jax.shard_map(
        functools.partial(on_device, mesh.shape["off"], mesh.shape["depth"]),
        mesh=mesh,
        in_specs=(
            P("off", None, "depth", None),
            P("off"),
            wave,
            wave,
            wave,
            P("off", "depth", None),
        ),
        out_specs=wave,
        check_vma=False,
    )
```

time: 20.9 us -> 16.6 us (0.79)
  the two profiles are of different devices: /device:TPU:0 before, /device:TPU:9 now
where the time goes in v2:
time: 16.6 us; the launch traced here: 16.5 us
  Pallas kernels  15.8 us (95%)
  local copies, waits for them, and re-layouts  0.66 us (4%)
    pallas_call x1, Pallas kernels, on_device(): pl.pallas_call(functools.partial(kernel, n, nd), out_shape=jax.ShapeDtype...  15.8 us
    unnamed x1, local copies, waits for them, and re-layouts  0.66 us

profile of v2, /device:TPU:9, one launch (start us, length us, event | category | flops | bytes accessed | tf_op | source)
XLA Modules:
  0.0 16.5 jit_solution(10049966016635657195)
XLA Ops:
  0.0 15.8 %born_step.1 = f32[1,8,16,256]{3,2,1,0:T(8,128)S(1)} custom-call(s32[16]{0:T(128)} %off_hbm.1, bf16[16,32,16,256]{3,2,1,0:T(8,128)(2,1)} %img_hbm.1, bf16[1,8,16,256]{3,2,1,0:T(8,128)(2,1)} %bg_hbm.1, f32[1,8,16,256]{3,2,1,0:T(8,128)} %now_hbm.1, f32[1,8,16,256]{3,2,1,0:T(8,128)} %prev_hbm.1, f32[8,16,256]{2,1,0:T(8,128)} %cour_hbm.1), custom_call_target="tpu_custom_call" | custom-call | tf_op jit(solution)/shard_map/born_step/pallas_call | solution.py:345
  15.8 0.7 %copy.8 = f32[1,8,16,256]{3,2,1,0:T(8,128)} copy(f32[1,8,16,256]{3,2,1,0:T(8,128)S(1)} %born_step.1) | data formatting | bytes 262144

commit v3 on v2

--- a/solution.py
+++ b/solution.py
@@ -19,11 +19,11 @@
     n, nd,
     off_hbm, img_hbm, bg_hbm, now_hbm, prev_hbm, cour_hbm,
     out_ref,
-    off_ref, img, raw, bg, wext, prev, cour, shift, acc,
-    part_out, part_in, scale_out, scale_in, tally,
-    edge_out, edge_in, edge_scale_out, edge_scale_in, edge_tally,
-    load_sem, img_sem, ready, near_ready, bg_recv, bg_send, fwd_send,
-    halo_send, halo_recv, p_recv, p_send,
+    off_ref, img, raw, bg, wext, local, shift, acc,
+    part_out, part_in, scale_out, scale_in, pend, join_in, join_scale, tally,
+    edge_out, edge_in, edge_scale_out, edge_scale_in, edge_tally, piece_tally,
+    load_sem, img_sem, ready, near_ready, bg_recv, bg_send,
+    halo_send, halo_recv, p_recv, join_recv, p_send,
 ):
     K, _, Z, X = img.shape
     Y = out_ref.shape[1]
@@ -45,8 +45,10 @@
     ld_off = pltpu.make_async_copy(off_hbm, off_ref, load_sem.at[1])
     ld_now = pltpu.make_async_copy(
         now_hbm.at[0], wext.at[pl.ds(R, Y), pl.ds(8, Z), :], load_sem.at[2])
+    prev, cour = local.at[0], local.at[1]
     ld_prev = pltpu.make_async_copy(prev_hbm.at[0], prev, load_sem.at[3])
-    ld_cour = pltpu.make_async_copy(cour_hbm, cour, load_sem.at[4])
+    ld_cour = pltpu.make_async_copy(cour_hbm, cour, load_sem.at[3])
+    ld_local = pltpu.make_async_copy(local, local, load_sem.at[3])
     ld_bg.start()
     ld_off.start()
     ld_now.start()
@@ -63,15 +65,18 @@
 
     def img_load(j):
         rows = pl.ds(j * Y, Y)
-        return pltpu.make_async_copy(img_hbm.at[:, rows], img.at[:, rows], img_sem.at[j])
+        sem = img_sem.at[jnp.where(j == me, 0, 1)]
+        return pltpu.make_async_copy(img_hbm.at[:, rows], img.at[:, rows], sem)
 
     def order(i):
+        mid = jnp.where(i == 0, 0, jnp.where(i == 1, n - 1, i))
+        rest = jnp.where(i < me, i - 1, i + 1)
         last = me == n - 1
-        rest = jnp.where(jnp.logical_or(i - 1 < me, last), i - 1, i + 1)
-        first = jnp.where(last, me - 1, me + 1)
-        high = jnp.where(i == 0, first, jnp.where(i == 1, 0, rest))
-        low = jnp.where(jnp.logical_and(i == 0, me == 1), 0, i + 1)
-        return jnp.where(me < 2, low, high)
+        first = jnp.where(last, me - 1, 0)
+        second = jnp.where(last, 0, me - 1)
+        high = jnp.where(i == 0, first, jnp.where(i == 1, second, rest))
+        low = jnp.where(i == 0, 2, jnp.where(i == 1, 1, i + 1))
+        return jnp.where(me == 0, low, jnp.where(me == 1, mid, high))
 
     img_load(me).start()
 
@@ -105,17 +110,20 @@
                      (edge_scale_out.at[num[side]], edge_scale_in.at[num[there]])]
         return [
             pltpu.make_async_remote_copy(
-                src_ref=src, dst_ref=dst, send_sem=halo_send.at[num[side]],
-                recv_sem=halo_recv.at[num[there]], device_id=near[side], device_id_type=MESH)
+                src_ref=src, dst_ref=dst, send_sem=halo_send.at[num[side] // 2],
+                recv_sem=halo_recv.at[num[side] // 2], device_id=near[side], device_id_type=MESH)
             for src, dst in pairs
         ]
 
-    def halo_wait(side, sem):
-        if side in "ud":
-            there = wext.at[edge[side][0], edge[side][1], :]
-            pltpu.make_async_copy(there, there, sem.at[num[side]]).wait()
-        else:
-            pltpu.make_async_copy(edge_tally, edge_tally, sem.at[num[side]]).wait()
+    def halo_wait(sem):
+        for axis, (low, high) in enumerate(("lr", "ud")):
+            count = has[low].astype(jnp.int32) + has[high].astype(jnp.int32)
+            for c in (1, 2):
+                whole = (edge_tally.at[pl.ds(0, c)], wext.at[pl.ds(R, Y), pl.ds(0, 8 * c), :])[axis]
+
+                @pl.when(count == c)
+                def _():
+                    pltpu.make_async_copy(whole, whole, sem.at[axis]).wait()
 
     lower = me + has["l"].astype(jnp.int32) + has["u"].astype(jnp.int32)
 
@@ -125,11 +133,11 @@
     for t in range(n - 1, 0, -1):
         @pl.when(me - t >= 0)
         def _():
-            pl.semaphore_signal(ready.at[me], inc=1, device_id=far(me - t), device_id_type=MESH)
-    for side, slot in (("l", 0), ("u", 1)):
+            pl.semaphore_signal(ready.at[me - 1], inc=1, device_id=far(me - t), device_id_type=MESH)
+    for side in "lu":
         @pl.when(has[side])
         def _():
-            pl.semaphore_signal(near_ready.at[slot], inc=1, device_id=near[side], device_id_type=MESH)
+            pl.semaphore_signal(near_ready.at[0], inc=1, device_id=near[side], device_id_type=MESH)
 
     @pl.when(has["u"])
     def _():
@@ -158,18 +166,31 @@
     def piece_of(j, c):
         return bg.at[j, pl.ds(c * step, step)]
 
-    def bg_copy(j, c, target, send):
+    def place(j, g):
+        return j - (j > g).astype(jnp.int32)
+
+    def bg_copy(j, c, target, slot, send):
         return pltpu.make_async_remote_copy(
             src_ref=piece_of(j, c), dst_ref=piece_of(j, c), send_sem=send,
-            recv_sem=bg_recv.at[j * pieces + c], device_id=target, device_id_type=MESH)
-
-    def bg_sent(j, target, send):
-        return pltpu.make_async_remote_copy(
-            src_ref=bg.at[j], dst_ref=bg.at[j], send_sem=send,
-            recv_sem=bg_recv.at[j * pieces], device_id=target, device_id_type=MESH)
+            recv_sem=bg_recv.at[slot * pieces + c], device_id=target, device_id_type=MESH)
+
+    def bg_sent(sem, count, most):
+        for c in range(1, most):
+            whole = bg.at[pl.ds(0, c)]
+
+            @pl.when(count == c)
+            def _():
+                pltpu.make_async_copy(whole, whole, sem).wait()
 
     def relayed(j, g):
-        return jnp.logical_and(j >= 1, g >= j + 2)
+        left = jnp.logical_and(g == 0, j >= 3)
+        right = jnp.logical_and(g >= j + 2, j >= 1)
+        return jnp.where(g < j, left, right)
+
+    def relay(j):
+        onward = jnp.where(j < me, me + 1, me - 1)
+        ok = jnp.logical_and(onward >= 0, onward < n)
+        return onward, jnp.logical_and(ok, relayed(j, onward))
 
     def direct(g):
         ok = jnp.logical_and(g >= 0, g < n)
@@ -177,9 +198,9 @@
 
     def send_own(g):
         for c in range(pieces):
-            bg_copy(me, c, far(g), bg_send.at[g]).start()
-
-    for t in range(1, n):
+            bg_copy(me, c, far(g), place(me, g), bg_send.at[0]).start()
+
+    for t in range(n - 1, 0, -1):
         @pl.when(direct(me - t))
         def _():
             send_own(me - t)
@@ -222,11 +243,22 @@
             total = term if total is None else total + term
         return total
 
+    joins = jnp.logical_and(me >= 1, me < n - 1)
+
     def part_send(j, c):
-        for s, (src, dst) in enumerate(((part_out, part_in), (scale_out, scale_in))):
-            pltpu.make_async_remote_copy(
-                src_ref=src.at[j, c], dst_ref=dst.at[me, c], send_sem=p_send.at[s],
-                recv_sem=p_recv.at[me], device_id=far(j), device_id_type=MESH).start()
+        def copies(dsts, recv, target):
+            for src, dst in zip((part_out, scale_out), dsts):
+                pltpu.make_async_remote_copy(
+                    src_ref=src.at[j, c], dst_ref=dst, send_sem=p_send.at[0],
+                    recv_sem=recv, device_id=target, device_id_type=MESH).start()
+
+        @pl.when(j == me + 2)
+        def _():
+            copies((join_in.at[c], join_scale.at[c]), join_recv.at[c], {"off": me + 1})
+
+        @pl.when(j != me + 2)
+        def _():
+            copies((part_in.at[me, c], scale_in.at[me, c]), p_recv.at[place(me, j)], far(j))
 
     img_load(me).wait()
     for c in range(pieces):
@@ -235,51 +267,65 @@
     for t in range(1, n):
         @pl.when(direct(me + t))
         def _():
-            pl.semaphore_wait(ready.at[me + t], 1)
+            pl.semaphore_wait(ready.at[me + t - 1], 1)
             send_own(me + t)
-    @pl.when(has["d"])
+
+    higher = has["r"].astype(jnp.int32) + has["d"].astype(jnp.int32)
+
+    @pl.when(higher > 0)
     def _():
-        pl.semaphore_wait(near_ready.at[1], 1)
-        for copy in halo_copies("d"):
-            copy.start()
-
-    @pl.when(has["r"])
-    def _():
-        pl.semaphore_wait(near_ready.at[0], 1)
-        for copy in halo_copies("r"):
-            copy.start()
+        pl.semaphore_wait(near_ready.at[0], higher)
+    for side in "rd":
+        @pl.when(has[side])
+        def _():
+            for copy in halo_copies(side):
+                copy.start()
+
+    rest = img.at[:, pl.ds(0, (n - 1) * Y)]
+    pltpu.make_async_copy(rest, rest, img_sem.at[1]).wait()
 
     @pl.loop(0, n - 1)
     def _(i):
         j = order(i)
 
-        onward = jnp.where(j < me, me + 1, me - 1)
-        go_on = jnp.logical_and(
-            jnp.logical_and(onward >= 0, onward < n), relayed(j, onward))
+        onward, go_on = relay(j)
         for c in range(pieces):
-            bg_copy(j, c, far(j), bg_send.at[j]).wait_recv()
+            bg_copy(j, c, far(j), place(j, me), bg_send.at[0]).wait_recv()
 
             @pl.when(go_on)
             def _():
-                bg_copy(j, c, {"off": onward}, fwd_send.at[j]).start()
+                bg_copy(j, c, {"off": onward}, place(j, onward), bg_send.at[1]).start()
 
             if c == 0:
-                img_load(j).wait()
-
                 @pl.when(jnp.logical_and(j > me, relayed(me, j)))
                 def _():
-                    pl.semaphore_wait(ready.at[j], 1)
-            encode(partial(j, c), part_out, scale_out, j, c)
-            part_send(j, c)
-
-    ld_prev.wait()
-    ld_cour.wait()
-    for side in "lrud":
-      @pl.when(has[side])
-      def _():
-          halo_wait(side, halo_recv)
-          if side in "lr":
-              wext[edge[side][0], edge[side][1], :] = decode(edge_in, edge_scale_in, num[side])
+                    pl.semaphore_wait(ready.at[j - 1], 1)
+            total = partial(j, c)
+            later = jnp.logical_and(joins, j == me + 1)
+
+            @pl.when(later)
+            def _():
+                pend[pl.ds(c * step, step)] = total
+
+            @pl.when(jnp.logical_not(later))
+            def _():
+                encode(total, part_out, scale_out, j, c)
+                part_send(j, c)
+
+    @pl.when(joins)
+    def _():
+        for c in range(pieces):
+            pltpu.make_async_copy(piece_tally, piece_tally, join_recv.at[c]).wait()
+            total = pend[pl.ds(c * step, step)] + decode(join_in, join_scale, c)
+            encode(total, part_out, scale_out, me + 1, c)
+            part_send(me + 1, c)
+
+    ld_local.wait()
+    halo_wait(halo_recv)
+    for side in "lr":
+        @pl.when(has[side])
+        def _():
+            wext[edge[side][0], edge[side][1], :] = decode(edge_in, edge_scale_in, num[side])
 
     wide = lax.broadcasted_iota(jnp.int32, (Z, X), 1)
 
@@ -302,35 +348,23 @@
     def _(i):
         j = order(i)
 
-        pltpu.make_async_copy(tally, tally, p_recv.at[j]).wait()
-        for c in range(pieces):
-            rows = pl.ds(c * step, step)
-            fin[rows] = fin[rows] + cour[rows] * decode(part_in, scale_in, j, c)
-
-    for side in "lrud":
-      @pl.when(has[side])
-      def _():
-          halo_wait(side, halo_send)
-    for t in range(1, n):
-      for g in (me - t, me + t):
-          @pl.when(direct(g))
-          def _():
-              bg_sent(me, far(g), bg_send.at[g]).wait_send()
-
-    @pl.loop(0, n - 1)
-    def _(i):
-      j = order(i)
-      onward = jnp.where(j < me, me + 1, me - 1)
-      go_on = jnp.logical_and(
-          jnp.logical_and(onward >= 0, onward < n), relayed(j, onward))
-
-      @pl.when(go_on)
-      def _():
-          bg_sent(j, {"off": onward}, fwd_send.at[j]).wait_send()
-
-    for s, src in enumerate((part_out, scale_out)):
-      sent = src.at[pl.ds(0, n - 1)]
-      pltpu.make_async_copy(sent, sent, p_send.at[s]).wait()
+
+        @pl.when(j != me - 2)
+        def _():
+            pltpu.make_async_copy(tally.at[0], tally.at[0], p_recv.at[place(j, me)]).wait()
+            for c in range(pieces):
+                rows = pl.ds(c * step, step)
+                fin[rows] = fin[rows] + cour[rows] * decode(part_in, scale_in, j, c)
+
+    halo_wait(halo_send)
+    sent, passed = 0, 0
+    for g in range(n):
+      there = g != me
+      sent = sent + jnp.logical_and(there, direct(g)).astype(jnp.int32)
+      passed = passed + jnp.logical_and(there, relay(g)[1]).astype(jnp.int32)
+    bg_sent(bg_send.at[0], sent, n)
+    bg_sent(bg_send.at[1], passed, n - 1)
+    pltpu.make_async_copy(tally, tally, p_send.at[0]).wait()
 
 
 def on_device(n, nd, image, offset_of, background, wave_now, wave_prev, courant):
@@ -353,23 +387,26 @@
             pltpu.VMEM((Y, Z, X), jnp.bfloat16),
             pltpu.VMEM((n, Y, Z, X), jnp.bfloat16),
             pltpu.VMEM((Y + 2 * R, Z + 16, X), f32),
-            pltpu.VMEM((Y, Z, X), f32),
-            pltpu.VMEM((Y, Z, X), f32),
+            pltpu.VMEM((2, Y, Z, X), f32),
             pltpu.VMEM(((K + 1) // 2, 2 * LANES, 2 * LANES), jnp.bfloat16),
             pltpu.VMEM((Y, Z, X), f32),
             pltpu.VMEM((n, pieces, step, Z, X), jnp.int16),
             pltpu.VMEM((n, pieces, step, Z, X), jnp.int16),
             pltpu.VMEM((n, pieces, 1, LANES), f32),
             pltpu.VMEM((n, pieces, 1, LANES), f32),
-            pltpu.VMEM((lines, LANES), f32),
+            pltpu.VMEM((Y, Z, X), f32),
+            pltpu.VMEM((pieces, step, Z, X), jnp.int16),
+            pltpu.VMEM((pieces, 1, LANES), f32),
+            pltpu.VMEM((n - 1, lines, LANES), f32),
             pltpu.VMEM((2, R, Z, X), jnp.int16),
             pltpu.VMEM((2, R, Z, X), jnp.int16),
             pltpu.VMEM((2, 1, LANES), f32),
             pltpu.VMEM((2, 1, LANES), f32),
-            pltpu.VMEM(((R * Z * X * 2) // (LANES * 4) + 1, LANES), f32),
-            dma((5,)), dma((n,)), regular((n,)), regular((2,)),
-            dma((n * pieces,)), dma((n,)), dma((n,)),
-            dma((4,)), dma((4,)), dma((n,)), dma((2,)),
+            pltpu.VMEM((2, (R * Z * X * 2) // (LANES * 4) + 1, LANES), f32),
+            pltpu.VMEM((lines // pieces, LANES), f32),
+            dma((4,)), dma((2,)), regular((n - 1,)), regular((1,)),
+            dma(((n - 1) * pieces,)), dma((2,)), dma((2,)), dma((2,)),
+            dma((n - 1,)), dma((pieces,)), dma((1,)),
         ],
         compiler_params=pltpu.CompilerParams(
             collective_id=0, has_side_effects=True, vmem_limit_bytes=50331648),

time: 16.6 us -> 15.9 us (0.958)
  the two profiles are of different devices: /device:TPU:9 before, /device:TPU:0 now
where the time goes in v3:
time: 15.9 us; the launch traced here: 15.7 us
  Pallas kernels  15.1 us (95%)
  local copies, waits for them, and re-layouts  0.66 us (4%)
    pallas_call x1, Pallas kernels, on_device(): pl.pallas_call(functools.partial(kernel, n, nd), out_shape=jax.ShapeDtype...  15.1 us
    unnamed x1, local copies, waits for them, and re-layouts  0.66 us

profile of v3, /device:TPU:0, one launch (start us, length us, event | category | flops | bytes accessed | tf_op | source)
XLA Modules:
  0.0 15.7 jit_solution(10863881536026810918)
XLA Ops:
  0.0 15.1 %born_step.1 = f32[1,8,16,256]{3,2,1,0:T(8,128)S(1)} custom-call(s32[16]{0:T(128)} %off_hbm.1, bf16[16,32,16,256]{3,2,1,0:T(8,128)(2,1)} %img_hbm.1, bf16[1,8,16,256]{3,2,1,0:T(8,128)(2,1)} %bg_hbm.1, f32[1,8,16,256]{3,2,1,0:T(8,128)} %now_hbm.1, f32[1,8,16,256]{3,2,1,0:T(8,128)} %prev_hbm.1, f32[8,16,256]{2,1,0:T(8,128)} %cour_hbm.1), custom_call_target="tpu_custom_call" | custom-call | tf_op jit(solution)/shard_map/born_step/pallas_call | solution.py:379
  15.1 0.7 %copy.8 = f32[1,8,16,256]{3,2,1,0:T(8,128)} copy(f32[1,8,16,256]{3,2,1,0:T(8,128)S(1)} %born_step.1) | data formatting | bytes 262144

commit v4 on v3

--- a/solution.py
+++ b/solution.py
@@ -32,7 +32,8 @@
     half = K * n // 2
     me = lax.axis_index("off")
     dep = lax.axis_index("depth")
-    other_shot = lax.axis_size("shot") - 1 - lax.axis_index("shot")
+    shot = lax.axis_index("shot")
+    other_shot = lax.axis_size("shot") - 1 - shot
     has = {"l": me > 0, "r": me < n - 1, "u": dep > 0, "d": dep < nd - 1}
     near = {"l": {"off": me - 1}, "r": {"off": me + 1},
             "u": {"depth": dep - 1}, "d": {"depth": dep + 1}}
@@ -182,7 +183,7 @@
             def _():
                 pltpu.make_async_copy(whole, whole, sem).wait()
 
-    def relayed(j, g):
+    def relayed(j, g, core):
         left = jnp.logical_and(g == 0, j >= 3)
         right = jnp.logical_and(g >= j + 2, j >= 1)
         return jnp.where(g < j, left, right)
@@ -190,11 +191,11 @@
     def relay(j):
         onward = jnp.where(j < me, me + 1, me - 1)
         ok = jnp.logical_and(onward >= 0, onward < n)
-        return onward, jnp.logical_and(ok, relayed(j, onward))
+        return onward, jnp.logical_and(ok, relayed(j, onward, other_shot))
 
     def direct(g):
         ok = jnp.logical_and(g >= 0, g < n)
-        return jnp.logical_and(ok, jnp.logical_not(relayed(me, g)))
+        return jnp.logical_and(ok, jnp.logical_not(relayed(me, g, shot)))
 
     def send_own(g):
         for c in range(pieces):
@@ -284,33 +285,66 @@
     rest = img.at[:, pl.ds(0, (n - 1) * Y)]
     pltpu.make_async_copy(rest, rest, img_sem.at[1]).wait()
 
-    @pl.loop(0, n - 1)
-    def _(i):
+    def laplace():
+        ld_local.wait()
+        halo_wait(halo_recv)
+        for side in "lr":
+            @pl.when(has[side])
+            def _():
+                wext[edge[side][0], edge[side][1], :] = decode(edge_in, edge_scale_in, num[side])
+
+        wide = lax.broadcasted_iota(jnp.int32, (Z, X), 1)
+
+        def plane(y, carry):
+            centre = wext[y + R, pl.ds(8, Z), :]
+            running = 3.0 * STENCIL[0] * centre
+            for r in range(1, R + 1):
+                beside = wext[y + R + r, pl.ds(8, Z), :] + wext[y + R - r, pl.ds(8, Z), :]
+                beside = beside + wext[y + R, pl.ds(8 + r, Z), :]
+                beside = beside + wext[y + R, pl.ds(8 - r, Z), :]
+                beside = beside + jnp.where(wide < X - r, pltpu.roll(centre, X - r, 1), 0.0)
+                beside = beside + jnp.where(wide >= r, pltpu.roll(centre, r, 1), 0.0)
+                running = running + STENCIL[r] * beside
+            fin[y] = 2.0 * centre - prev[y] + cour[y] * (running + acc[y])
+            return carry
+
+        lax.fori_loop(0, Y, plane, 0)
+
+    early = jnp.logical_and(me >= 2, me < n - 1)
+
+    @pl.loop(0, (n - 1) * pieces)
+    def _(q):
+        swap = jnp.where(q == 0, pieces, jnp.where(q <= pieces, q - 1, q))
+        turns = jnp.where(q == 1, 2, jnp.where(q == 2, 1, q)) if pieces == 2 and n > 2 else q
+        q = jnp.where(early, swap, jnp.where(me == 1, turns, q))
+        i, c = q // pieces, q % pieces
         j = order(i)
 
+        @pl.when(jnp.logical_and(me == 0, q == (n - 2) * pieces))
+        def _():
+            laplace()
+
         onward, go_on = relay(j)
-        for c in range(pieces):
-            bg_copy(j, c, far(j), place(j, me), bg_send.at[0]).wait_recv()
-
-            @pl.when(go_on)
-            def _():
-                bg_copy(j, c, {"off": onward}, place(j, onward), bg_send.at[1]).start()
-
-            if c == 0:
-                @pl.when(jnp.logical_and(j > me, relayed(me, j)))
-                def _():
-                    pl.semaphore_wait(ready.at[j - 1], 1)
-            total = partial(j, c)
-            later = jnp.logical_and(joins, j == me + 1)
-
-            @pl.when(later)
-            def _():
-                pend[pl.ds(c * step, step)] = total
-
-            @pl.when(jnp.logical_not(later))
-            def _():
-                encode(total, part_out, scale_out, j, c)
-                part_send(j, c)
+        bg_copy(j, c, far(j), place(j, me), bg_send.at[0]).wait_recv()
+
+        @pl.when(go_on)
+        def _():
+            bg_copy(j, c, {"off": onward}, place(j, onward), bg_send.at[1]).start()
+
+        @pl.when(jnp.logical_and(c == 0, jnp.logical_and(j > me, relayed(me, j, shot))))
+        def _():
+            pl.semaphore_wait(ready.at[j - 1], 1)
+        total = partial(j, c)
+        later = jnp.logical_and(joins, j == me + 1)
+
+        @pl.when(later)
+        def _():
+            pend[pl.ds(c * step, step)] = total
+
+        @pl.when(jnp.logical_not(later))
+        def _():
+            encode(total, part_out, scale_out, j, c)
+            part_send(j, c)
 
     @pl.when(joins)
     def _():
@@ -320,34 +354,28 @@
             encode(total, part_out, scale_out, me + 1, c)
             part_send(me + 1, c)
 
-    ld_local.wait()
-    halo_wait(halo_recv)
-    for side in "lr":
-        @pl.when(has[side])
-        def _():
-            wext[edge[side][0], edge[side][1], :] = decode(edge_in, edge_scale_in, num[side])
-
-    wide = lax.broadcasted_iota(jnp.int32, (Z, X), 1)
-
-    def plane(y, carry):
-        centre = wext[y + R, pl.ds(8, Z), :]
-        running = 3.0 * STENCIL[0] * centre
-        for r in range(1, R + 1):
-            beside = wext[y + R + r, pl.ds(8, Z), :] + wext[y + R - r, pl.ds(8, Z), :]
-            beside = beside + wext[y + R, pl.ds(8 + r, Z), :]
-            beside = beside + wext[y + R, pl.ds(8 - r, Z), :]
-            beside = beside + jnp.where(wide < X - r, pltpu.roll(centre, X - r, 1), 0.0)
-            beside = beside + jnp.where(wide >= r, pltpu.roll(centre, r, 1), 0.0)
-            running = running + STENCIL[r] * beside
-        fin[y] = 2.0 * centre - prev[y] + cour[y] * (running + acc[y])
-        return carry
-
-    lax.fori_loop(0, Y, plane, 0)
+    @pl.when(me > 0)
+    def _():
+        laplace()
+
+    def drain():
+        halo_wait(halo_send)
+        sent, passed = 0, 0
+        for g in range(n):
+          there = g != me
+          sent = sent + jnp.logical_and(there, direct(g)).astype(jnp.int32)
+          passed = passed + jnp.logical_and(there, relay(g)[1]).astype(jnp.int32)
+        bg_sent(bg_send.at[0], sent, n)
+        bg_sent(bg_send.at[1], passed, n - 1)
+        pltpu.make_async_copy(tally, tally, p_send.at[0]).wait()
 
     @pl.loop(0, n - 1)
     def _(i):
         j = order(i)
 
+        @pl.when(i == n - 2)
+        def _():
+            drain()
 
         @pl.when(j != me - 2)
         def _():
@@ -355,16 +383,6 @@
             for c in range(pieces):
                 rows = pl.ds(c * step, step)
                 fin[rows] = fin[rows] + cour[rows] * decode(part_in, scale_in, j, c)
-
-    halo_wait(halo_send)
-    sent, passed = 0, 0
-    for g in range(n):
-      there = g != me
-      sent = sent + jnp.logical_and(there, direct(g)).astype(jnp.int32)
-      passed = passed + jnp.logical_and(there, relay(g)[1]).astype(jnp.int32)
-    bg_sent(bg_send.at[0], sent, n)
-    bg_sent(bg_send.at[1], passed, n - 1)
-    pltpu.make_async_copy(tally, tally, p_send.at[0]).wait()
 
 
 def on_device(n, nd, image, offset_of, background, wave_now, wave_prev, courant):

time: 15.9 us -> 17.4 us (1.094)
  Pallas kernels: 15.1 us -> 16.6 us
    pallas_call x1, Pallas kernels: 15.1 us -> 16.6 us  [on_device(): pl.pallas_call(functools.partial(kernel, n, nd), out_shape=jax.ShapeDtype...]
where the time goes in v4:
time: 17.4 us; the launch traced here: 17.3 us
  Pallas kernels  16.6 us (95%)
  local copies, waits for them, and re-layouts  0.66 us (4%)
    pallas_call x1, Pallas kernels, on_device(): pl.pallas_call(functools.partial(kernel, n, nd), out_shape=jax.ShapeDtype...  16.6 us
    unnamed x1, local copies, waits for them, and re-layouts  0.66 us

profile of v4, /device:TPU:0, one launch (start us, length us, event | category | flops | bytes accessed | tf_op | source)
XLA Modules:
  0.0 17.3 jit_solution(14732068476581296783)
XLA Ops:
  0.0 16.6 %born_step.1 = f32[1,8,16,256]{3,2,1,0:T(8,128)S(1)} custom-call(s32[16]{0:T(128)} %off_hbm.1, bf16[16,32,16,256]{3,2,1,0:T(8,128)(2,1)} %img_hbm.1, bf16[1,8,16,256]{3,2,1,0:T(8,128)(2,1)} %bg_hbm.1, f32[1,8,16,256]{3,2,1,0:T(8,128)} %now_hbm.1, f32[1,8,16,256]{3,2,1,0:T(8,128)} %prev_hbm.1, f32[8,16,256]{2,1,0:T(8,128)} %cour_hbm.1), custom_call_target="tpu_custom_call" | custom-call | tf_op jit(solution)/shard_map/born_step/pallas_call | solution.py:397
  16.6 0.7 %copy.8 = f32[1,8,16,256]{3,2,1,0:T(8,128)} copy(f32[1,8,16,256]{3,2,1,0:T(8,128)S(1)} %born_step.1) | data formatting | bytes 262144

commit v5 on v4

--- a/solution.py
+++ b/solution.py
@@ -310,7 +310,7 @@
 
         lax.fori_loop(0, Y, plane, 0)
 
-    early = jnp.logical_and(me >= 2, me < n - 1)
+    early = jnp.logical_and(jnp.logical_and(me >= 2, me < n - 1), shot == 0)
 
     @pl.loop(0, (n - 1) * pieces)
     def _(q):

time: 17.4 us -> 15.7 us (0.902)
  Pallas kernels: 16.6 us -> 14.9 us
    pallas_call x1, Pallas kernels: 16.6 us -> 14.9 us  [on_device(): pl.pallas_call(functools.partial(kernel, n, nd), out_shape=jax.ShapeDtype...]
where the time goes in v5:
time: 15.7 us; the launch traced here: 15.5 us
  Pallas kernels  14.9 us (95%)
  local copies, waits for them, and re-layouts  0.66 us (4%)
    pallas_call x1, Pallas kernels, on_device(): pl.pallas_call(functools.partial(kernel, n, nd), out_shape=jax.ShapeDtype...  14.9 us
    unnamed x1, local copies, waits for them, and re-layouts  0.66 us

profile of v5, /device:TPU:0, one launch (start us, length us, event | category | flops | bytes accessed | tf_op | source)
XLA Modules:
  0.0 15.5 jit_solution(10843918994069671074)
XLA Ops:
  0.0 14.9 %born_step.1 = f32[1,8,16,256]{3,2,1,0:T(8,128)S(1)} custom-call(s32[16]{0:T(128)} %off_hbm.1, bf16[16,32,16,256]{3,2,1,0:T(8,128)(2,1)} %img_hbm.1, bf16[1,8,16,256]{3,2,1,0:T(8,128)(2,1)} %bg_hbm.1, f32[1,8,16,256]{3,2,1,0:T(8,128)} %now_hbm.1, f32[1,8,16,256]{3,2,1,0:T(8,128)} %prev_hbm.1, f32[8,16,256]{2,1,0:T(8,128)} %cour_hbm.1), custom_call_target="tpu_custom_call" | custom-call | tf_op jit(solution)/shard_map/born_step/pallas_call | solution.py:397
  14.9 0.7 %copy.8 = f32[1,8,16,256]{3,2,1,0:T(8,128)} copy(f32[1,8,16,256]{3,2,1,0:T(8,128)S(1)} %born_step.1) | data formatting | bytes 262144

commit v6 on v5

--- a/solution.py
+++ b/solution.py
@@ -177,7 +177,7 @@
 
     def bg_sent(sem, count, most):
         for c in range(1, most):
-            whole = bg.at[pl.ds(0, c)]
+            whole = bg.at[pl.ds(0, c)] if c <= n else img.at[pl.ds(0, 2), pl.ds(0, c * Y // 2)]
 
             @pl.when(count == c)
             def _():
@@ -315,7 +315,9 @@
     @pl.loop(0, (n - 1) * pieces)
     def _(q):
         swap = jnp.where(q == 0, pieces, jnp.where(q <= pieces, q - 1, q))
-        turns = jnp.where(q == 1, 2, jnp.where(q == 2, 1, q)) if pieces == 2 and n > 2 else q
+        turns = q
+        if pieces == 2 and n > 2:
+            turns = jnp.where(shot == 0, jnp.where(q < 4, (q // 2) + 2 * (1 - q % 2), q), q)
         q = jnp.where(early, swap, jnp.where(me == 1, turns, q))
         i, c = q // pieces, q % pieces
         j = order(i)
@@ -329,7 +331,7 @@
 
         @pl.when(go_on)
         def _():
-            bg_copy(j, c, {"off": onward}, place(j, onward), bg_send.at[1]).start()
+            bg_copy(j, c, {"off": onward}, place(j, onward), bg_send.at[0]).start()
 
         @pl.when(jnp.logical_and(c == 0, jnp.logical_and(j > me, relayed(me, j, shot))))
         def _():
@@ -365,8 +367,7 @@
           there = g != me
           sent = sent + jnp.logical_and(there, direct(g)).astype(jnp.int32)
           passed = passed + jnp.logical_and(there, relay(g)[1]).astype(jnp.int32)
-        bg_sent(bg_send.at[0], sent, n)
-        bg_sent(bg_send.at[1], passed, n - 1)
+        bg_sent(bg_send.at[0], sent + passed, 2 * n)
         pltpu.make_async_copy(tally, tally, p_send.at[0]).wait()
 
     @pl.loop(0, n - 1)
@@ -423,7 +424,7 @@
             pltpu.VMEM((2, (R * Z * X * 2) // (LANES * 4) + 1, LANES), f32),
             pltpu.VMEM((lines // pieces, LANES), f32),
             dma((4,)), dma((2,)), regular((n - 1,)), regular((1,)),
-            dma(((n - 1) * pieces,)), dma((2,)), dma((2,)), dma((2,)),
+            dma(((n - 1) * pieces,)), dma((1,)), dma((2,)), dma((2,)),
             dma((n - 1,)), dma((pieces,)), dma((1,)),
         ],
         compiler_params=pltpu.CompilerParams(

time: 15.7 us -> 15.7 us (level)
  no operation moved by 1% of the time
where the time goes in v6:
time: 15.7 us; the launch traced here: 15.5 us
  Pallas kernels  14.8 us (94%)
  local copies, waits for them, and re-layouts  0.66 us (4%)
    pallas_call x1, Pallas kernels, on_device(): pl.pallas_call(functools.partial(kernel, n, nd), out_shape=jax.ShapeDtype...  14.8 us
    unnamed x1, local copies, waits for them, and re-layouts  0.66 us

profile of v6, /device:TPU:0, one launch (start us, length us, event | category | flops | bytes accessed | tf_op | source)
XLA Modules:
  0.0 15.5 jit_solution(3706795688051674718)
XLA Ops:
  0.0 14.8 %born_step.1 = f32[1,8,16,256]{3,2,1,0:T(8,128)S(1)} custom-call(s32[16]{0:T(128)} %off_hbm.1, bf16[16,32,16,256]{3,2,1,0:T(8,128)(2,1)} %img_hbm.1, bf16[1,8,16,256]{3,2,1,0:T(8,128)(2,1)} %bg_hbm.1, f32[1,8,16,256]{3,2,1,0:T(8,128)} %now_hbm.1, f32[1,8,16,256]{3,2,1,0:T(8,128)} %prev_hbm.1, f32[8,16,256]{2,1,0:T(8,128)} %cour_hbm.1), custom_call_target="tpu_custom_call" | custom-call | tf_op jit(solution)/shard_map/born_step/pallas_call | solution.py:398
  14.9 0.7 %copy.8 = f32[1,8,16,256]{3,2,1,0:T(8,128)} copy(f32[1,8,16,256]{3,2,1,0:T(8,128)S(1)} %born_step.1) | data formatting | bytes 262144
